TPU v7x, 32 devices: a whole 2x2x4 slice. The times are simulated.
32 devices in a mesh: dp: 8 (over z, y), tensor: 4 (over x, core).
Axes of the slice: x: 2, y: 2, z: 4, core: 2. Of those that a mesh axis runs over, the one named last changes fastest.
Arguments:
- block_input: bfloat16 [2048, 8, 768], P('tensor', 'dp'), may hold values from -6 to 6
- condition: bfloat16 [8, 128], P('dp'), may hold values from -6 to 6
- modulation_weight: bfloat16 [128, 4608], P(None, 'dp'), may hold values from -0.25 to 0.25
- modulation_bias: bfloat16 [4608], P('dp'), may hold values from -3 to 3
- first_gain: bfloat16 [768], P('dp'), may hold values from 0.5 to 1.5
- qkv_weight: bfloat16 [3, 768, 768], P(None, 'dp', 'tensor'), may hold values from -0.3125 to 0.3125
- out_weight: bfloat16 [768, 768], P('tensor', 'dp'), may hold values from -0.875 to 0.875
- second_gain: bfloat16 [768], P('dp'), may hold values from 0.5 to 1.5
- up_weight: bfloat16 [768, 3072], P('dp', 'tensor'), may hold values from -0.21875 to 0.21875
- up_bias: bfloat16 [3072], P('dp'), may hold values from -3 to 3
- down_weight: bfloat16 [3072, 768], P('tensor', 'dp'), may hold values from -0.109375 to 0.109375
- down_bias: bfloat16 [768], P('dp'), may hold values from -2 to 2
- grad_output: bfloat16 [2048, 8, 768], P('tensor', 'dp'), may hold values from -6 to 6
Outputs:
- block_output: bfloat16 [2048, 8, 768], P('tensor', 'dp')
- grad_input: float32 [2048, 8, 768], P('tensor', 'dp')
- grad_condition: float32 [8, 128], P('dp')
- grad_modulation_weight: float32 [128, 4608], replicated
- grad_modulation_bias: float32 [4608], replicated
- grad_first_gain: float32 [768], replicated
- grad_qkv_weight: float32 [3, 768, 768], P(None, 'dp', 'tensor')
- grad_out_weight: float32 [768, 768], P('tensor', 'dp')
- grad_second_gain: float32 [768], replicated
- grad_up_weight: float32 [768, 3072], P('dp', 'tensor')
- grad_up_bias: float32 [3072], replicated
- grad_down_weight: float32 [3072, 768], P('tensor', 'dp')
- grad_down_bias: float32 [768], replicated
- root_means: float32 [3], replicated
All inputs are finite; a program needn't handle non-finite values.
Results may differ from a plain program's by a relative error of at most 0.014.
The roundings to bfloat16 on the way count: a program that leaves them out, or rounds other values in their place, can miss the bound.
Values may be sent and summed in bfloat16 or wider, within the bound.
A program may use at most 128 MiB of HBM per device.

v0:
```python
from functools import partial
import jax
import jax.numpy as jnp
from jax import lax
from jax.sharding import PartitionSpec as P

HEAD_DIM = 64
PRECISE = lax.Precision.HIGHEST
EPSILON = 1e-05


def norm_mod(stream, gain_vec, shift_vec, scale_vec):
    row_mean = jnp.mean(stream, axis=-1, keepdims=True)
    centred = stream - row_mean
    variance = jnp.mean(centred * centred, axis=-1, keepdims=True)
    normed = centred * lax.rsqrt(variance + EPSILON) * gain_vec
    return normed * (1.0 + scale_vec) + shift_vec


def rotary_tables(length, head_width):
    half_dim = head_width // 2
    inverse = 1.0 / 10000.0 ** (jnp.arange(half_dim, dtype=jnp.float32) * 2.0 / head_width)
    angles = jnp.arange(length, dtype=jnp.float32)[:, None] * inverse[None, :]
    angles = jnp.concatenate([angles, angles], axis=-1)
    return (jnp.cos(angles), jnp.sin(angles))


def rotate(vector, cos_table, sine_table):
    half_dim = vector.shape[-1] // 2
    turned = jnp.concatenate([-vector[..., half_dim:], vector[..., :half_dim]], axis=-1)
    return vector * cos_table[:, None, None, :] + turned * sine_table[:, None, None, :]


def gelu_tanh(values):
    return jax.nn.gelu(values, approximate=True)


def seq_block(heads_all, sequence, offset, block_rows):
    whole_seq = lax.dynamic_index_in_dim(heads_all, sequence, 0, keepdims=False)
    return lax.dynamic_slice_in_dim(whole_seq, offset, block_rows, 1)


def blocks_to_rows(blocks, sequences, per_seq, length):
    heads_here, block_rows, head_width = (blocks.shape[1], blocks.shape[2], blocks.shape[3])
    arranged = blocks.reshape(sequences, per_seq, heads_here, block_rows, head_width).transpose(
        1, 3, 0, 2, 4
    )
    return arranged.reshape(length, sequences, heads_here, head_width)


def shards(
    block_input,
    condition,
    modulation_weight,
    modulation_bias,
    first_gain,
    qkv_weight,
    out_weight,
    second_gain,
    up_weight,
    up_bias,
    down_weight,
    down_bias,
    grad_output,
):
    n_tensor = lax.axis_size("tensor")
    n_data = lax.axis_size("dp")
    t_index = lax.axis_index("tensor")
    d_index = lax.axis_index("dp")
    local_rows, sequences, features = block_input.shape
    length = local_rows * n_tensor
    ada_full, ada_b_full, gain_one, qkv_w, out_w, gain_two, up_w, b_up_full, down_w, b_down_full = (
        lax.all_gather(modulation_weight, "dp", axis=1, tiled=True),
        lax.all_gather(modulation_bias, "dp", axis=0, tiled=True),
        lax.all_gather(first_gain, "dp", axis=0, tiled=True),
        lax.all_gather(qkv_weight, "dp", axis=1, tiled=True),
        lax.all_gather(out_weight, "dp", axis=1, tiled=True),
        lax.all_gather(second_gain, "dp", axis=0, tiled=True),
        lax.all_gather(up_weight, "dp", axis=0, tiled=True),
        lax.all_gather(up_bias, "dp", axis=0, tiled=True),
        lax.all_gather(down_weight, "dp", axis=1, tiled=True),
        lax.all_gather(down_bias, "dp", axis=0, tiled=True),
    )
    ada_float = ada_full.astype(jnp.float32)
    gain_one_f = gain_one.astype(jnp.float32)
    gain_two_f = gain_two.astype(jnp.float32)
    b_up_f = b_up_full.astype(jnp.float32)
    b_down_f = b_down_full.astype(jnp.float32)
    cond_float = condition.astype(jnp.float32)
    modulation = jnp.dot(cond_float, ada_float, precision=PRECISE) + ada_b_full.astype(jnp.float32)
    shift_attn, scale_attn, gate_attn, shift_mlp, scale_mlp, gate_mlp = jnp.split(
        modulation, 6, axis=-1
    )
    stream = block_input.astype(jnp.float32)
    attn_in = norm_mod(stream, gain_one_f, shift_attn, scale_attn).astype(jnp.bfloat16)
    full_attn_in = lax.all_gather(attn_in, "tensor", axis=0, tiled=True)
    projected = jnp.einsum("lbd,jde->lbje", full_attn_in, qkv_w, preferred_element_type=jnp.float32)
    heads_here = qkv_w.shape[2] // HEAD_DIM
    head_shape = (length, sequences, heads_here, HEAD_DIM)
    cos_table, sine_table = rotary_tables(length, HEAD_DIM)
    query_scale = HEAD_DIM ** (-0.5)
    query_pre = projected[:, :, 0].reshape(head_shape)
    key_pre = projected[:, :, 1].reshape(head_shape)
    query_rot = (rotate(query_pre, cos_table, sine_table) * query_scale).astype(jnp.bfloat16)
    key_rot = rotate(key_pre, cos_table, sine_table).astype(jnp.bfloat16)
    value_low = projected[:, :, 2].reshape(head_shape).astype(jnp.bfloat16)
    query_heads = query_rot.transpose(1, 2, 0, 3)
    key_heads = key_rot.transpose(1, 2, 0, 3)
    value_heads = value_low.transpose(1, 2, 0, 3)
    block_rows = min(512, length)
    per_seq = length // block_rows
    block_count = sequences * per_seq

    def forward_block(position):
        sequence = position // per_seq
        offset = position % per_seq * block_rows
        query_blk = seq_block(query_heads, sequence, offset, block_rows)
        key_seq = lax.dynamic_index_in_dim(key_heads, sequence, 0, keepdims=False)
        value_seq = lax.dynamic_index_in_dim(value_heads, sequence, 0, keepdims=False)
        scores = jnp.einsum("hqe,hke->hqk", query_blk, key_seq, preferred_element_type=jnp.float32)
        row_max = jnp.max(scores, axis=-1, keepdims=True)
        shifted = jnp.exp(scores - row_max)
        row_total = jnp.sum(shifted, axis=-1, keepdims=True)
        probs = (shifted / row_total).astype(jnp.bfloat16)
        mixed_blk = jnp.einsum("hqk,hke->hqe", probs, value_seq, preferred_element_type=jnp.float32)
        return (mixed_blk.astype(jnp.bfloat16), (row_max + jnp.log(row_total))[..., 0])

    mixed_blocks, log_total = lax.map(forward_block, jnp.arange(block_count))
    mixed_all = blocks_to_rows(mixed_blocks, sequences, per_seq, length).reshape(
        length, sequences, heads_here * HEAD_DIM
    )
    portion = mixed_all
    attn_out = lax.psum_scatter(
        jnp.einsum("lbe,ed->lbd", portion, out_w, preferred_element_type=jnp.float32),
        "tensor",
        scatter_dimension=0,
        tiled=True,
    )
    attn_branch = gate_attn * attn_out
    middle = stream + attn_branch
    mlp_in = norm_mod(middle, gain_two_f, shift_mlp, scale_mlp).astype(jnp.bfloat16)
    unit_count = up_w.shape[1]
    b_up_own = lax.dynamic_slice_in_dim(b_up_f, t_index * unit_count, unit_count, 0)
    full_mlp_in = lax.all_gather(mlp_in, "tensor", axis=0, tiled=True)
    hidden = (
        jnp.einsum("lbd,df->lbf", full_mlp_in, up_w, preferred_element_type=jnp.float32) + b_up_own
    )
    active = gelu_tanh(hidden).astype(jnp.bfloat16)
    portion = active
    mlp_out = (
        lax.psum_scatter(
            jnp.einsum("lbf,fd->lbd", portion, down_w, preferred_element_type=jnp.float32).astype(
                jnp.bfloat16
            ),
            "tensor",
            scatter_dimension=0,
            tiled=True,
        ).astype(jnp.float32)
        + b_down_f
    )
    mlp_branch = gate_mlp * mlp_out
    result = middle + mlp_branch
    local_squares = jnp.stack(
        [
            jnp.sum(attn_branch * attn_branch),
            jnp.sum(mlp_branch * mlp_branch),
            jnp.sum(result * result),
        ]
    )
    out_grad = grad_output.astype(jnp.float32)
    d_gate_mlp = jnp.sum(out_grad * mlp_out, axis=0)
    d_mlp = (gate_mlp * out_grad).astype(jnp.bfloat16)
    d_b_down = jnp.sum(d_mlp.astype(jnp.float32), axis=(0, 1))
    full_d_mlp = lax.all_gather(d_mlp, "tensor", axis=0, tiled=True)
    d_active = jnp.einsum("lbd,fd->lbf", full_d_mlp, down_w, preferred_element_type=jnp.float32)
    grad_down = jnp.einsum("lbf,lbd->fd", active, full_d_mlp, preferred_element_type=jnp.float32)
    d_hidden = jax.vjp(gelu_tanh, hidden)[1](d_active)[0].astype(jnp.bfloat16)
    grad_up = jnp.einsum("lbd,lbf->df", full_mlp_in, d_hidden, preferred_element_type=jnp.float32)
    own_b_up = jnp.sum(d_hidden.astype(jnp.float32), axis=(0, 1))
    d_b_up = lax.dynamic_update_slice_in_dim(
        jnp.zeros(b_up_f.shape, jnp.float32), own_b_up, t_index * unit_count, 0
    )
    portion = d_hidden
    d_mlp_in = lax.psum_scatter(
        jnp.einsum("lbf,df->lbd", portion, up_w, preferred_element_type=jnp.float32),
        "tensor",
        scatter_dimension=0,
        tiled=True,
    )
    pull_two = jax.vjp(norm_mod, middle, gain_two_f, shift_mlp, scale_mlp)[1]
    middle_part, d_gain_two, d_shift_mlp, d_scale_mlp = pull_two(d_mlp_in)
    d_middle = out_grad + middle_part
    d_gate_attn = jnp.sum(d_middle * attn_out, axis=0)
    d_attn = (gate_attn * d_middle).astype(jnp.bfloat16)
    full_d_attn = lax.all_gather(d_attn, "tensor", axis=0, tiled=True)
    grad_out = jnp.einsum("lbe,lbd->ed", mixed_all, full_d_attn, preferred_element_type=jnp.float32)
    d_mixed = jnp.einsum(
        "lbd,ed->lbe", full_d_attn, out_w, preferred_element_type=jnp.float32
    ).astype(jnp.bfloat16)
    d_mixed_heads = d_mixed.reshape(head_shape).transpose(1, 2, 0, 3)

    def backward_block(accums, inputs):
        key_acc, value_acc = accums
        position, log_blk = inputs
        sequence = position // per_seq
        offset = position % per_seq * block_rows
        query_blk = seq_block(query_heads, sequence, offset, block_rows)
        d_mixed_blk = seq_block(d_mixed_heads, sequence, offset, block_rows)
        key_seq = lax.dynamic_index_in_dim(key_heads, sequence, 0, keepdims=False)
        value_seq = lax.dynamic_index_in_dim(value_heads, sequence, 0, keepdims=False)
        scores = jnp.einsum("hqe,hke->hqk", query_blk, key_seq, preferred_element_type=jnp.float32)
        probs = jnp.exp(scores - log_blk[..., None])
        d_probs = jnp.einsum(
            "hqe,hke->hqk", d_mixed_blk, value_seq, preferred_element_type=jnp.float32
        )
        row_inner = jnp.sum(probs * d_probs, axis=-1, keepdims=True)
        d_scores = (probs * (d_probs - row_inner)).astype(jnp.bfloat16)
        d_query_blk = jnp.einsum(
            "hqk,hke->hqe", d_scores, key_seq, preferred_element_type=jnp.float32
        )
        d_key_blk = jnp.einsum(
            "hqk,hqe->hke", d_scores, query_blk, preferred_element_type=jnp.float32
        )
        d_value_blk = jnp.einsum(
            "hqk,hqe->hke",
            probs.astype(jnp.bfloat16),
            d_mixed_blk,
            preferred_element_type=jnp.float32,
        )
        key_now = lax.dynamic_index_in_dim(key_acc, sequence, 0, keepdims=False) + d_key_blk
        value_now = lax.dynamic_index_in_dim(value_acc, sequence, 0, keepdims=False) + d_value_blk
        key_acc = lax.dynamic_update_index_in_dim(key_acc, key_now, sequence, 0)
        value_acc = lax.dynamic_update_index_in_dim(value_acc, value_now, sequence, 0)
        return ((key_acc, value_acc), d_query_blk)

    zero_heads = jnp.zeros((sequences, heads_here, length, HEAD_DIM), jnp.float32)
    (d_key_heads, d_value_heads), d_query_blocks = lax.scan(
        backward_block, (zero_heads, zero_heads), (jnp.arange(block_count), log_total)
    )
    d_query_rot = blocks_to_rows(d_query_blocks, sequences, per_seq, length) * query_scale
    pull_rotate = jax.vjp(partial(rotate, cos_table=cos_table, sine_table=sine_table), query_pre)[1]
    d_query_pre = pull_rotate(d_query_rot)[0]
    d_key_pre = pull_rotate(d_key_heads.transpose(2, 0, 1, 3))[0]
    d_value_all = d_value_heads.transpose(2, 0, 1, 3)
    flat_shape = (length, sequences, heads_here * HEAD_DIM)
    d_projected = jnp.stack(
        [
            d_query_pre.reshape(flat_shape),
            d_key_pre.reshape(flat_shape),
            d_value_all.reshape(flat_shape),
        ],
        axis=2,
    ).astype(jnp.bfloat16)
    grad_qkv = jnp.einsum(
        "lbd,lbje->jde", full_attn_in, d_projected, preferred_element_type=jnp.float32
    )
    portion = d_projected
    d_attn_in = lax.psum_scatter(
        jnp.einsum("lbje,jde->lbd", portion, qkv_w, preferred_element_type=jnp.float32),
        "tensor",
        scatter_dimension=0,
        tiled=True,
    )
    pull_one = jax.vjp(norm_mod, stream, gain_one_f, shift_attn, scale_attn)[1]
    stream_part, d_gain_one, d_shift_attn, d_scale_attn = pull_one(d_attn_in)
    d_stream = d_middle + stream_part
    grad_qkv_own, grad_out_own, grad_up_own, grad_down_own = (
        lax.psum_scatter(grad_qkv, "dp", scatter_dimension=1, tiled=True),
        lax.psum_scatter(grad_out, "dp", scatter_dimension=1, tiled=True),
        lax.psum_scatter(grad_up, "dp", scatter_dimension=0, tiled=True),
        lax.psum_scatter(grad_down, "dp", scatter_dimension=1, tiled=True),
    )
    d_modulation = jnp.concatenate(
        [d_shift_attn, d_scale_attn, d_gate_attn, d_shift_mlp, d_scale_mlp, d_gate_mlp], axis=-1
    )
    d_ada_b = jnp.sum(d_modulation, axis=0)
    d_ada_w = jnp.dot(cond_float.T, d_modulation, precision=PRECISE)
    d_cond_here = jnp.dot(d_modulation, ada_float.T, precision=PRECISE)
    cond_table = jnp.zeros((sequences * n_data, condition.shape[1]), jnp.float32)
    cond_table = lax.dynamic_update_slice_in_dim(cond_table, d_cond_here, d_index * sequences, 0)
    totals = lax.psum(
        (local_squares, cond_table, d_ada_w, d_ada_b, d_gain_one, d_gain_two, d_b_up, d_b_down),
        ("dp", "tensor"),
    )
    root_means = jnp.sqrt(totals[0] / (local_rows * sequences * features * n_tensor * n_data))
    grad_condition = lax.dynamic_slice_in_dim(totals[1], d_index * sequences, sequences, 0)
    return (
        result.astype(jnp.bfloat16),
        d_stream,
        grad_condition,
        totals[2],
        totals[3],
        totals[4],
        grad_qkv_own,
        grad_out_own,
        totals[5],
        grad_up_own,
        totals[6],
        grad_down_own,
        totals[7],
        root_means,
    )


def solution(mesh):
    in_specs = (
        P("tensor", "dp", None),
        P("dp", None),
        P(None, "dp"),
        P("dp"),
        P("dp"),
        P(None, "dp", "tensor"),
        P("tensor", "dp"),
        P("dp"),
        P("dp", "tensor"),
        P("dp"),
        P("tensor", "dp"),
        P("dp"),
        P("tensor", "dp", None),
    )
    out_specs = (
        P("tensor", "dp", None),
        P("tensor", "dp", None),
        P("dp", None),
        P(),
        P(),
        P(),
        P(None, "dp", "tensor"),
        P("tensor", "dp"),
        P(),
        P("dp", "tensor"),
        P(),
        P("tensor", "dp"),
        P(),
        P(),
    )
    return jax.shard_map(shards, mesh=mesh, in_specs=in_specs, out_specs=out_specs, check_vma=False)
```

profile of v0, /device:TPU:0, one launch (start us, length us, event | category | flops | bytes accessed | tf_op | source)
XLA Modules:
  0.0 1209.0 jit_solution(3161789117916995180)
XLA Ops:
  13.9 39.8 %all-reduce.9 = (bf16[4608]{0:T(1024)(128)(2,1)S(1)}, bf16[768]{0:T(1024)(128)(2,1)S(1)}, bf16[768]{0:T(1024)(128)(2,1)}, bf16[768]{0:T(1024)(128)(2,1)}) all-reduce(bf16[4608]{0:T(1024)(128)(2,1)S(1)} %dynamic-update-slice, bf16[768]{0:T(1024)(128)(2,1)S(1)} %dynamic-update-slice.1, ...), channel_id=1, replica_groups=mesh['dp'=8,'tensor'=4] {'dp'}, use_global_device_ids=true, to_apply=%add.4 | all-reduce | flops 6912 | bytes 27648
  60.7 34.8 %all_gather.46 = bf16[3,768,192]{2,0,1:T(4,128)(2,1)S(1)} all-gather(bf16[3,96,192]{2,0,1:T(4,128)(2,1)S(1)} %copy.49), channel_id=1, replica_groups=mesh['dp'=8,'tensor'=4] {'dp'}, dimensions={1}, use_global_device_ids=true | all-gather | bytes 995328 | tf_op jit(solution)/shard_map/all_gather | solution.py:76
  97.6 33.3 %all_gather.47 = bf16[192,768]{0,1:T(8,128)(2,1)} all-gather(bf16[192,96]{0,1:T(8,128)(2,1)S(1)} %copy.55), channel_id=1, replica_groups=mesh['dp'=8,'tensor'=4] {'dp'}, dimensions={1}, use_global_device_ids=true | all-gather | bytes 331776 | tf_op jit(solution)/shard_map/all_gather | solution.py:77
  146.7 101.9 %while.30 = (s32[]{:T(128)}, bf16[4,3,512,64]{3,2,1,0:T(8,128)(2,1)}, f32[4,3,512]{2,1,0:T(4,128)}, s32[4]{0:T(128)S(1)}, bf16[1,3,2048,64]{2,3,1,0:T(8,128)(2,1...) while((s32[]{:T(128)}, ...), condition=%wide.region_5.6_spmd, body=%wide.region_2.5_spmd.sunk | while | flops 1217493504 | bytes 29923640 | solution.py:128
  151.1 14.6 %dot_general.129 = f32[3,512,64]{2,1,0:T(8,128)} custom-call(bf16[3,512,64]{2,1,0:T(8,128)(2,1)} %bitcast.231, bf16[3,2048,64]{2,1,0:T(8,128)(2,1)S(1)} %bitcast.227, bf16[3,2048,64]{2,1,0:T(8,128)(2,1)} %bitcast.230), custom_call_target="tpu_custom_call" | custom-call | flops 805306368 | bytes 1769472 | tf_op jit(solution)/shard_map/while/body/eval_jaxpr/hqk,hke->hqe/dot_general | solution.py:125
  176.6 14.7 %dot_general.129 = f32[3,512,64]{2,1,0:T(8,128)} custom-call(bf16[3,512,64]{2,1,0:T(8,128)(2,1)} %bitcast.231, bf16[3,2048,64]{2,1,0:T(8,128)(2,1)S(1)} %bitcast.227, bf16[3,2048,64]{2,1,0:T(8,128)(2,1)} %bitcast.230), custom_call_target="tpu_custom_call" | custom-call | flops 805306368 | bytes 1769472 | tf_op jit(solution)/shard_map/while/body/eval_jaxpr/hqk,hke->hqe/dot_general | solution.py:125
  202.1 14.7 %dot_general.129 = f32[3,512,64]{2,1,0:T(8,128)} custom-call(bf16[3,512,64]{2,1,0:T(8,128)(2,1)} %bitcast.231, bf16[3,2048,64]{2,1,0:T(8,128)(2,1)S(1)} %bitcast.227, bf16[3,2048,64]{2,1,0:T(8,128)(2,1)} %bitcast.230), custom_call_target="tpu_custom_call" | custom-call | flops 805306368 | bytes 1769472 | tf_op jit(solution)/shard_map/while/body/eval_jaxpr/hqk,hke->hqe/dot_general | solution.py:125
  227.5 14.7 %dot_general.129 = f32[3,512,64]{2,1,0:T(8,128)} custom-call(bf16[3,512,64]{2,1,0:T(8,128)(2,1)} %bitcast.231, bf16[3,2048,64]{2,1,0:T(8,128)(2,1)S(1)} %bitcast.227, bf16[3,2048,64]{2,1,0:T(8,128)(2,1)} %bitcast.230), custom_call_target="tpu_custom_call" | custom-call | flops 805306368 | bytes 1769472 | tf_op jit(solution)/shard_map/while/body/eval_jaxpr/hqk,hke->hqe/dot_general | solution.py:125
  256.4 56.3 %reduce-scatter.13.cloned.1.call-done = f32[512,1,768]{2,0,1:T(8,128)} async-done(((f32[2048,1,768]{2,0,1:T(8,128)}), f32[512,1,768]{2,0,1:T(8,128)}) %reduce-scatter.13.cloned.1.call-update) | async-done | bytes 1572880 | tf_op jit(solution)/shard_map/reduce_scatter | solution.py:133
  319.7 26.1 %all-gather = bf16[8,1,384]{2,1,0:T(2,128)(2,1)S(1)} all-gather(bf16[1,1,384]{2,1,0:T(2,128)(2,1)S(1)} %reshape.555), channel_id=1, replica_groups=mesh['dp'=8,'tensor'=4] {'dp'}, dimensions={0}, use_global_device_ids=true | all-gather | bytes 6912 | tf_op jit(solution)/shard_map/all_gather | solution.py:80
  347.7 8.4 all-gather.15.cloned.1.call-done
  356.1 29.4 %all-gather.13.cloned.1.call-done = bf16[2048,1,768]{2,0,1:T(8,128)(2,1)} async-done(((bf16[512,1,768]{2,0,1:T(8,128)(2,1)}), bf16[2048,1,768]{2,0,1:T(8,128)(2,1)}) %all-gather.13.cloned.1.call-update) | async-done | bytes 3145744 | tf_op jit(solution)/shard_map/all_gather | solution.py:144
  385.5 7.5 fusion.51
  393.0 35.9 %all-gather.17.cloned.1.call-done = bf16[768,768]{0,1:T(8,128)(2,1)} async-done(((bf16[768,96]{0,1:T(8,128)(2,1)}), bf16[768,768]{0,1:T(8,128)(2,1)}) %all-gather.17.cloned.1.call-update) | async-done | bytes 1179664 | tf_op jit(solution)/shard_map/all_gather | solution.py:81
  428.9 8.9 fusion.55
  437.9 20.6 %all-gather.19.cloned.1.call-done = bf16[2048,1,768]{2,0,1:T(8,128)(2,1)} async-done(((bf16[512,1,768]{2,0,1:T(8,128)(2,1)}), bf16[2048,1,768]{2,0,1:T(8,128)(2,1)}) %all-gather.19.cloned.1.call-update) | async-done | bytes 3145744 | tf_op jit(solution)/shard_map/all_gather | solution.py:174
  458.4 9.4 convert_reduce_fusion
  469.6 4.5 convolution_bitcast_fusion.3
  475.6 23.6 %reduce-scatter.15.cloned.1.call-done = bf16[512,1,768]{2,0,1:T(8,128)(2,1)} async-done(((bf16[2048,1,768]{2,0,1:T(8,128)(2,1)}), bf16[512,1,768]{2,0,1:T(8,128)(2,1)}) %reduce-scatter.15.cloned.1.call-update) | async-done | bytes 786448 | tf_op jit(solution)/shard_map/reduce_scatter | solution.py:151
  499.1 60.9 %reduce-scatter.17.cloned.1.call-done = f32[512,1,768]{2,0,1:T(8,128)} async-done(((f32[2048,1,768]{2,0,1:T(8,128)}), f32[512,1,768]{2,0,1:T(8,128)}) %reduce-scatter.17.cloned.1.call-update) | async-done | bytes 1572880 | tf_op jit(solution)/shard_map/reduce_scatter | solution.py:184
  560.1 4.8 multiply_reduce_fusion.2
  569.5 28.6 %all-gather.21.cloned.1.call-done = bf16[2048,1,768]{2,0,1:T(8,128)(2,1)} async-done(((bf16[512,1,768]{2,0,1:T(8,128)(2,1)}), bf16[2048,1,768]{2,0,1:T(8,128)(2,1)}) %all-gather.21.cloned.1.call-update) | async-done | bytes 3145744 | tf_op jit(solution)/shard_map/all_gather | solution.py:195
  603.6 110.1 %while.31 = (s32[]{:T(128)}, f32[1,3,2048,64]{2,3,1,0:T(8,128)S(1)}, f32[1,3,2048,64]{2,3,1,0:T(8,128)}, f32[4,3,512,64]{2,3,1,0:T(8,128)}, s32[4]{0:T(128)S(1)}...) while((s32[]{:T(128)}, ...), condition=%wide.region_15.16_spmd, body=%wide.region_13.15_spmd.sunk | while | flops 2042362368 | bytes 129411448 | solution.py:237
  609.7 4.9 fusion.154
  614.5 4.0 multiply_reduce_fusion.10
  618.5 4.5 multiply_convert_fusion.6
  623.1 5.7 fusion.155
  637.2 4.9 fusion.154
  642.1 4.0 multiply_reduce_fusion.10
  646.1 4.5 multiply_convert_fusion.6
  650.6 5.7 fusion.155
  664.7 4.9 fusion.154
  673.6 4.5 multiply_convert_fusion.6
  678.1 5.7 fusion.155
  692.2 4.9 fusion.154
  701.1 4.5 multiply_convert_fusion.6
  705.7 5.7 fusion.155
  716.6 4.2 fusion.89
  738.5 6.7 convolution_bitcast_fusion.1
  745.9 8.7 fusion.45
  755.0 6.0 fusion.49
  764.0 19.5 %reduce-scatter.27.cloned.1.call-done = f32[96,192]{1,0:T(8,128)} async-done(((f32[768,192]{1,0:T(8,128)}), f32[96,192]{1,0:T(8,128)}) %reduce-scatter.27.cloned.1.call-update) | async-done | bytes 73744
  785.1 68.1 %reduce-scatter.25.cloned.1.call-done = f32[96,576]{1,0:T(8,128)} async-done(((f32[768,576]{1,0:T(8,128)}), f32[96,576]{1,0:T(8,128)}) %reduce-scatter.25.cloned.1.call-update) | async-done | bytes 221200
  855.2 58.1 %reduce-scatter.19.cloned.1.call-done = f32[512,1,768]{2,0,1:T(8,128)} async-done(((f32[2048,1,768]{2,0,1:T(8,128)}), f32[512,1,768]{2,0,1:T(8,128)}) %reduce-scatter.19.cloned.1.call-update) | async-done | bytes 1572880 | tf_op jit(solution)/shard_map/reduce_scatter | solution.py:258
  925.0 41.4 %all-reduce.8 = (f32[8,128]{1,0:T(8,128)S(1)}, f32[4608]{0:T(1024)}, f32[768]{0:T(1024)}, f32[768]{0:T(1024)}, f32[3072]{0:T(1024)}, /*index=5*/f32[768]{0:T(1024)}, f32[3]{0:T(128)S(1)}) all-reduce(f32[8,128]{1,0:T(8,128)S(1)} %dynamic_update_slice.30, f32[4608]{0:T(1024)S(1)} %reduce.25, ...), channel_id=1, replica_groups=mesh['dp'=8,'tensor'=4] {'dp','tensor'}, use_global_device_ids=true, to_apply=%region_25.26 | all-reduce | flops 11011 | bytes 88088 | tf_op jit(solution)/shard_map/psum | solution.py:281
  967.4 19.2 %reduce-scatter.23.cloned.1.call-done = f32[768,96]{0,1:T(8,128)} async-done(((f32[768,768]{0,1:T(8,128)}), f32[768,96]{0,1:T(8,128)}) %reduce-scatter.23.cloned.1.call-update) | async-done | bytes 294928 | tf_op jit(solution)/shard_map/reduce_scatter | solution.py:271
  986.7 72.0 %reduce-scatter.21.cloned.1.call-done = f32[96,768]{1,0:T(8,128)} async-done(((f32[768,768]{1,0:T(8,128)}), f32[96,768]{1,0:T(8,128)}) %reduce-scatter.21.cloned.1.call-update) | async-done | bytes 294928 | tf_op jit(solution)/shard_map/reduce_scatter | solution.py:270
  1058.7 140.1 %all-reduce.12.cloned.1.call-done = f32[128,4608]{1,0:T(8,128)} async-done(((f32[128,4608]{1,0:T(8,128)}), f32[128,4608]{1,0:T(8,128)}) %all-reduce.12.cloned.1.call-update) | async-done | bytes 2359312 | tf_op jit(solution)/shard_map/psum | solution.py:281
  (308 shorter events, 172.5 us)
Async XLA Ops:
  7.2 49.4 %copy-start.57 = (bf16[1,128]{1,0:T(2,128)(2,1)S(1)}, bf16[1,128]{1,0:T(2,128)(2,1)}, u32[]{:S(2)}) copy-start(bf16[1,128]{1,0:T(2,128)(2,1)} %param.18) | copy-start | bytes 772
  7.2 51.8 %copy-start.3 = (bf16[512,1,768]{2,0,1:T(8,128)(2,1)S(1)}, bf16[512,1,768]{2,0,1:T(8,128)(2,1)}, u32[]{:S(2)}) copy-start(bf16[512,1,768]{2,0,1:T(8,128)(2,1)} %param.17) | copy-start | bytes 2359300
  7.2 49.4 %all-gather.9.cloned.1.call-start = ((), (), s32[]{:S(2)}) async-start(), calls=%async_computation.8 | async-start | bytes 1327104 | tf_op jit(solution)/shard_map/all_gather | solution.py:73
  7.9 126.0 %all-gather.11.cloned.1.call-start = ((), (), s32[]{:S(2)}) async-start(), calls=%async_computation.9 | async-start | bytes 3932160 | tf_op jit(solution)/shard_map/all_gather | solution.py:96
  53.7 6.6 copy-start.30
  55.0 5.3 copy-start.34
  56.6 3.8 copy-start.40
  56.6 3.9 copy-start.36
  58.3 2.2 copy-start.29
  59.0 253.7 %copy-start.37 = (f32[768]{0:T(1024)}, f32[768]{0:T(1024)S(1)}, u32[]{:S(2)}) copy-start(f32[768]{0:T(1024)S(1)} %get-tuple-element.319) | copy-start | bytes 9220
  60.3 252.4 %reduce-scatter.13.cloned.1.call-start = ((), (), s32[]{:S(2)}) async-start(), calls=%async_computation.10 | async-start | bytes 7864320 | tf_op jit(solution)/shard_map/reduce_scatter | solution.py:133
  97.6 36.4 %copy-start.23 = (bf16[3,768,192]{1,2,0:T(8,128)(2,1)S(1)}, bf16[3,768,192]{1,2,0:T(8,128)(2,1)}, u32[]{:S(2)}) copy-start(bf16[3,768,192]{1,2,0:T(8,128)(2,1)} %copy.50) | copy-start | bytes 2654212
  248.6 3.0 copy-start.20
  255.3 100.8 %all-gather.15.cloned.1.call-start = ((), (), s32[]{:S(2)}) async-start(), calls=%async_computation.12 | async-start | bytes 1327104 | tf_op jit(solution)/shard_map/all_gather | solution.py:79
  255.9 129.6 %all-gather.13.cloned.1.call-start = ((), (), s32[]{:S(2)}) async-start(), calls=%async_computation.11 | async-start | bytes 3932160 | tf_op jit(solution)/shard_map/all_gather | solution.py:144
  316.6 112.3 %all-gather.17.cloned.1.call-start = ((), (), s32[]{:S(2)}) async-start(), calls=%async_computation.13 | async-start | bytes 1327104 | tf_op jit(solution)/shard_map/all_gather | solution.py:81
  317.2 141.2 %all-gather.19.cloned.1.call-start = ((), (), s32[]{:S(2)}) async-start(), calls=%async_computation.15 | async-start | bytes 3932160 | tf_op jit(solution)/shard_map/all_gather | solution.py:174
  318.9 180.2 %reduce-scatter.15.cloned.1.call-start = ((), (), s32[]{:S(2)}) async-start(), calls=%async_computation.14 | async-start | bytes 3932160 | tf_op jit(solution)/shard_map/reduce_scatter | solution.py:151
  437.8 122.3 %reduce-scatter.17.cloned.1.call-start = ((), (), s32[]{:S(2)}) async-start(), calls=%async_computation.16 | async-start | bytes 7864320 | tf_op jit(solution)/shard_map/reduce_scatter | solution.py:184
  458.4 11.1 copy-start.61
  474.1 124.1 %all-gather.21.cloned.1.call-start = ((), (), s32[]{:S(2)}) async-start(), calls=%async_computation.17 | async-start | bytes 3932160 | tf_op jit(solution)/shard_map/all_gather | solution.py:195
  560.1 5.5 copy-start.12
  567.1 2.3 copy-start.7
  567.1 2.3 copy-start.42
  569.5 214.0 %reduce-scatter.27.cloned.1.call-start = ((), (), s32[]{:S(2)}) async-start(), calls=%async_computation.23 | async-start | bytes 884736
  623.1 5.7 copy-start
  650.6 5.7 copy-start
  678.1 5.7 copy-start
  705.7 5.7 copy-start
  713.8 2.8 copy-start.14
  716.6 4.5 copy-start.22
  720.8 132.4 %reduce-scatter.25.cloned.1.call-start = ((), (), s32[]{:S(2)}) async-start(), calls=%async_computation.22 | async-start | bytes 2211840
  726.0 2.2 copy-start.59
  737.2 176.1 %reduce-scatter.19.cloned.1.call-start = ((), (), s32[]{:S(2)}) async-start(), calls=%async_computation.18 | async-start | bytes 7864320 | tf_op jit(solution)/shard_map/reduce_scatter | solution.py:258
  745.3 241.4 %reduce-scatter.23.cloned.1.call-start = ((), (), s32[]{:S(2)}) async-start(), calls=%async_computation.21 | async-start | bytes 2654208 | tf_op jit(solution)/shard_map/reduce_scatter | solution.py:271
  745.9 9.0 copy-start.60
  754.7 304.0 %reduce-scatter.21.cloned.1.call-start = ((), (), s32[]{:S(2)}) async-start(), calls=%async_computation.20 | async-start | bytes 2654208 | tf_op jit(solution)/shard_map/reduce_scatter | solution.py:270
  761.0 152.3 %copy-start.4 = (bf16[512,1,768]{2,0,1:T(8,128)(2,1)S(1)}, bf16[512,1,768]{2,0,1:T(8,128)(2,1)}, u32[]{:S(2)}) copy-start(bf16[512,1,768]{2,0,1:T(8,128)(2,1)} %param.17) | copy-start | bytes 2359300
  761.0 152.3 %copy-start.31 = (f32[768]{0:T(1024)S(1)}, f32[768]{0:T(1024)}, u32[]{:S(2)}) copy-start(f32[768]{0:T(1024)} %copy-done.30) | copy-start | bytes 9220
  761.0 152.3 %copy-start.33 = (f32[768]{0:T(1024)S(1)}, f32[768]{0:T(1024)}, u32[]{:S(2)}) copy-start(f32[768]{0:T(1024)} %copy-done.32) | copy-start | bytes 9220
  761.0 152.3 %copy-start.35 = (f32[512]{0:T(512)S(1)}, f32[512]{0:T(512)}, u32[]{:S(2)}) copy-start(f32[512]{0:T(512)} %copy-done.34) | copy-start | bytes 6148
  761.1 437.7 %all-reduce.12.cloned.1.call-start = ((), (), s32[]{:S(2)}) async-start(), calls=%async_computation.19 | async-start | bytes 4718592 | tf_op jit(solution)/shard_map/psum | solution.py:281
  854.4 60.9 %copy-start.45 = (f32[512]{0:T(512)S(1)}, f32[512]{0:T(512)}, u32[]{:S(2)}) copy-start(f32[512]{0:T(512)} %copy-done.44) | copy-start | bytes 6148
  854.4 60.9 %copy-start.41 = (f32[512]{0:T(512)S(1)}, f32[512]{0:T(512)}, u32[]{:S(2)}) copy-start(f32[512]{0:T(512)} %copy-done.40) | copy-start | bytes 6148
  913.3 2.1 copy-start.5
  921.5 2.8 copy-start.19
  921.5 3.4 copy-start.47
  921.6 3.4 copy-start.48
  (34 other events, 43.3 us)
Sparse Core Ops, SparseCore 0:
  10.2 44.0 all-gather.8
  60.4 25.7 all-gather.10
  255.4 57.2 reduce-scatter.12
  315.0 41.0 all-gather.14
  358.2 27.2 all-gather.12
  387.8 41.0 all-gather.16
  431.1 27.2 all-gather.18
  461.1 37.9 reduce-scatter.14
  501.7 58.3 reduce-scatter.16
  569.6 28.5 all-gather.20
  720.9 62.4 reduce-scatter.26
  787.4 65.8 reduce-scatter.24
  855.9 57.2 reduce-scatter.18
  917.2 69.4 reduce-scatter.22
  990.6 68.0 reduce-scatter.20
  1064.7 134.0 all-reduce.11
where the time goes:
time: 1210 us
  waiting for transfers between devices  643 us (53%)
  blocking collectives  175 us (14%)
  matrix products  160 us (13%)
  other arithmetic  77 us (6%)
  local copies, waits for them, and re-layouts  61.4 us (5%)
  Pallas kernels  58.6 us (5%)
  between operations  16.6 us (1%)
  loops' own time  15.9 us (1%)
    psum x1, waiting for transfers between devices, shards(): lax.psum((local_squares, cond_table, d_ada_w, d_ada_b, d_gain_one, d_gain...  140 us
    unnamed x18, waiting for transfers between devices  89.6 us
    reduce_scatter x1, waiting for transfers between devices, shards(): lax.psum_scatter(grad_up, 'dp', scatter_dimension=0, tiled=True)  72 us
    reduce_scatter x1, waiting for transfers between devices, shards(): lax.psum_scatter(jnp.einsum('lbf,df->lbd', portion, up_w, preferred_eleme...  60.9 us
    dot_general x4, Pallas kernels, forward_block(): jnp.einsum('hqk,hke->hqe', probs, value_seq, preferred_element_type=jnp.f...  58.6 us
    reduce_scatter x1, waiting for transfers between devices, shards(): lax.psum_scatter(jnp.einsum('lbje,jde->lbd', portion, qkv_w, preferred_el...  58.1 us
    reduce_scatter x1, waiting for transfers between devices, shards(): lax.psum_scatter(jnp.einsum('lbe,ed->lbd', portion, out_w, preferred_elem...  56.3 us
    psum x1, blocking collectives, shards(): lax.psum((local_squares, cond_table, d_ada_w, d_ada_b, d_gain_one, d_gain...  41.4 us
  transfers between devices with their start and end apart: 16, of which 14 were waited for; matrix products, arithmetic and copies ran while one was open for 9% of the time, Pallas kernels for 0%

commit v1 on v0

--- a/solution.py
+++ b/solution.py
@@ -192,7 +192,23 @@
     d_middle = out_grad + middle_part
     d_gate_attn = jnp.sum(d_middle * attn_out, axis=0)
     d_attn = (gate_attn * d_middle).astype(jnp.bfloat16)
-    full_d_attn = lax.all_gather(d_attn, "tensor", axis=0, tiled=True)
+    ways, here, step = (lax.axis_size("tensor"), lax.axis_index("tensor"), d_attn.shape[0])
+    shape = [n * ways if d == 0 else n for d, n in enumerate(d_attn.shape)]
+    full = lax.dynamic_update_slice_in_dim(
+        jnp.zeros(shape, d_attn.dtype), d_attn, here * step, axis=0
+    )
+    going_up = going_down = d_attn
+    for far in range(1, ways // 2 + 1):
+        going_up = lax.ppermute(going_up, "tensor", [(d, (d + 1) % ways) for d in range(ways)])
+        full = lax.dynamic_update_slice_in_dim(full, going_up, (here - far) % ways * step, axis=0)
+        if 2 * far < ways:
+            going_down = lax.ppermute(
+                going_down, "tensor", [(d, (d - 1) % ways) for d in range(ways)]
+            )
+            full = lax.dynamic_update_slice_in_dim(
+                full, going_down, (here + far) % ways * step, axis=0
+            )
+    full_d_attn = full
     grad_out = jnp.einsum("lbe,lbd->ed", mixed_all, full_d_attn, preferred_element_type=jnp.float32)
     d_mixed = jnp.einsum(
         "lbd,ed->lbe", full_d_attn, out_w, preferred_element_type=jnp.float32

time: 1210 us -> 1220 us (level)
    unnamed x18 -> x17, waiting for transfers between devices: 89.6 us -> 127 us
    reduce_scatter x1, waiting for transfers between devices: 58.1 us -> 22.9 us  [shards(): lax.psum_scatter(jnp.einsum('lbje,jde->lbd', portion, qkv_w, preferred_el...]
    all_gather x1 -> x0, waiting for transfers between devices: 28.6 us -> none  [shards(): full_d_attn = lax.all_gather(d_attn, 'tensor', axis=0, tiled=True)]
    ppermute x0 -> x3, waiting for transfers between devices: none -> 27.3 us  [the longest x2 27.3 us: shards(): lax.ppermute(going_up, 'tensor', [(d, (d + 1) % ways) for d in range(ways)])]
    unnamed x149 -> x145, local copies, waits for them, and re-layouts: 32.1 us -> 36.4 us
  transfers between devices with their start and end apart: 16 -> 18, of which waited for: 14 -> 15; matrix products, arithmetic and copies ran while one was open for 9% -> 9% of each run, Pallas kernels for 0% -> 0%
where the time goes in v1:
time: 1220 us
  waiting for transfers between devices  646 us (53%)
  blocking collectives  175 us (14%)
  matrix products  160 us (13%)
  other arithmetic  75.6 us (6%)
  local copies, waits for them, and re-layouts  67.4 us (6%)
  Pallas kernels  58.6 us (5%)
  between operations  16.5 us (1%)
  loops' own time  15.9 us (1%)
    psum x1, waiting for transfers between devices, shards(): lax.psum((local_squares, cond_table, d_ada_w, d_ada_b, d_gain_one, d_gain...  140 us
    unnamed x17, waiting for transfers between devices  127 us
    reduce_scatter x1, waiting for transfers between devices, shards(): lax.psum_scatter(grad_up, 'dp', scatter_dimension=0, tiled=True)  72 us
    reduce_scatter x1, waiting for transfers between devices, shards(): lax.psum_scatter(jnp.einsum('lbf,df->lbd', portion, up_w, preferred_eleme...  60.9 us
    dot_general x4, Pallas kernels, forward_block(): jnp.einsum('hqk,hke->hqe', probs, value_seq, preferred_element_type=jnp.f...  58.6 us
    reduce_scatter x1, waiting for transfers between devices, shards(): lax.psum_scatter(jnp.einsum('lbe,ed->lbd', portion, out_w, preferred_elem...  56.7 us
    psum x1, blocking collectives, shards(): lax.psum((local_squares, cond_table, d_ada_w, d_ada_b, d_gain_one, d_gain...  41.5 us
    unnamed x1, blocking collectives  39.8 us
  transfers between devices with their start and end apart: 18, of which 15 were waited for; matrix products, arithmetic and copies ran while one was open for 9% of the time, Pallas kernels for 0%

profile of v1, /device:TPU:0, one launch (start us, length us, event | category | flops | bytes accessed | tf_op | source)
XLA Modules:
  0.0 1219.3 jit_solution(15635840758009118727)
XLA Ops:
  13.9 39.8 %all-reduce.9 = (bf16[4608]{0:T(1024)(128)(2,1)S(1)}, bf16[768]{0:T(1024)(128)(2,1)S(1)}, bf16[768]{0:T(1024)(128)(2,1)S(1)}, bf16[768]{0:T(1024)(128)(2,1)}) all-reduce(bf16[4608]{0:T(1024)(128)(2,1)S(1)} %dynamic-update-slice, bf16[768]{0:T(1024)(128)(2,1)S(1)} %dynamic-update-slice.1, ...), channel_id=1, replica_groups=mesh['dp'=8,'tensor'=4] {'dp'}, use_global_device_ids=true, to_apply=%add.4 | all-reduce | flops 6912 | bytes 27648
  60.7 34.3 %all_gather.43 = bf16[3,768,192]{2,0,1:T(4,128)(2,1)S(1)} all-gather(bf16[3,96,192]{2,0,1:T(4,128)(2,1)S(1)} %copy.49), channel_id=1, replica_groups=mesh['dp'=8,'tensor'=4] {'dp'}, dimensions={1}, use_global_device_ids=true | all-gather | bytes 995328 | tf_op jit(solution)/shard_map/all_gather | solution.py:76
  97.1 33.5 %all_gather.44 = bf16[192,768]{0,1:T(8,128)(2,1)} all-gather(bf16[192,96]{0,1:T(8,128)(2,1)S(1)} %copy.55), channel_id=1, replica_groups=mesh['dp'=8,'tensor'=4] {'dp'}, dimensions={1}, use_global_device_ids=true | all-gather | bytes 331776 | tf_op jit(solution)/shard_map/all_gather | solution.py:77
  146.4 101.9 %while.30 = (s32[]{:T(128)}, bf16[4,3,512,64]{3,2,1,0:T(8,128)(2,1)}, f32[4,3,512]{2,1,0:T(4,128)}, s32[4]{0:T(128)S(1)}, bf16[1,3,2048,64]{2,3,1,0:T(8,128)(2,1...) while((s32[]{:T(128)}, ...), condition=%wide.region_5.6_spmd, body=%wide.region_2.5_spmd.sunk | while | flops 1217493504 | bytes 29923640 | solution.py:128
  150.8 14.7 %dot_general.129 = f32[3,512,64]{2,1,0:T(8,128)} custom-call(bf16[3,512,64]{2,1,0:T(8,128)(2,1)} %bitcast.232, bf16[3,2048,64]{2,1,0:T(8,128)(2,1)S(1)} %bitcast.228, bf16[3,2048,64]{2,1,0:T(8,128)(2,1)} %bitcast.231), custom_call_target="tpu_custom_call" | custom-call | flops 805306368 | bytes 1769472 | tf_op jit(solution)/shard_map/while/body/eval_jaxpr/hqk,hke->hqe/dot_general | solution.py:125
  176.3 14.7 %dot_general.129 = f32[3,512,64]{2,1,0:T(8,128)} custom-call(bf16[3,512,64]{2,1,0:T(8,128)(2,1)} %bitcast.232, bf16[3,2048,64]{2,1,0:T(8,128)(2,1)S(1)} %bitcast.228, bf16[3,2048,64]{2,1,0:T(8,128)(2,1)} %bitcast.231), custom_call_target="tpu_custom_call" | custom-call | flops 805306368 | bytes 1769472 | tf_op jit(solution)/shard_map/while/body/eval_jaxpr/hqk,hke->hqe/dot_general | solution.py:125
  201.8 14.7 %dot_general.129 = f32[3,512,64]{2,1,0:T(8,128)} custom-call(bf16[3,512,64]{2,1,0:T(8,128)(2,1)} %bitcast.232, bf16[3,2048,64]{2,1,0:T(8,128)(2,1)S(1)} %bitcast.228, bf16[3,2048,64]{2,1,0:T(8,128)(2,1)} %bitcast.231), custom_call_target="tpu_custom_call" | custom-call | flops 805306368 | bytes 1769472 | tf_op jit(solution)/shard_map/while/body/eval_jaxpr/hqk,hke->hqe/dot_general | solution.py:125
  227.2 14.7 %dot_general.129 = f32[3,512,64]{2,1,0:T(8,128)} custom-call(bf16[3,512,64]{2,1,0:T(8,128)(2,1)} %bitcast.232, bf16[3,2048,64]{2,1,0:T(8,128)(2,1)S(1)} %bitcast.228, bf16[3,2048,64]{2,1,0:T(8,128)(2,1)} %bitcast.231), custom_call_target="tpu_custom_call" | custom-call | flops 805306368 | bytes 1769472 | tf_op jit(solution)/shard_map/while/body/eval_jaxpr/hqk,hke->hqe/dot_general | solution.py:125
  256.1 56.7 %reduce-scatter.13.cloned.1.call-done = f32[512,1,768]{2,0,1:T(8,128)} async-done(((f32[2048,1,768]{2,0,1:T(8,128)}), f32[512,1,768]{2,0,1:T(8,128)}) %reduce-scatter.13.cloned.1.call-update) | async-done | bytes 1572880 | tf_op jit(solution)/shard_map/reduce_scatter | solution.py:133
  320.4 26.1 %all-gather = bf16[8,1,384]{2,1,0:T(2,128)(2,1)S(1)} all-gather(bf16[1,1,384]{2,1,0:T(2,128)(2,1)S(1)} %reshape.572), channel_id=1, replica_groups=mesh['dp'=8,'tensor'=4] {'dp'}, dimensions={0}, use_global_device_ids=true | all-gather | bytes 6912 | tf_op jit(solution)/shard_map/all_gather | solution.py:80
  348.5 7.7 all-gather.14.cloned.1.call-done
  356.1 29.4 %all-gather.12.cloned.1.call-done = bf16[2048,1,768]{2,0,1:T(8,128)(2,1)} async-done(((bf16[512,1,768]{2,0,1:T(8,128)(2,1)}), bf16[2048,1,768]{2,0,1:T(8,128)(2,1)}) %all-gather.12.cloned.1.call-update) | async-done | bytes 3145744 | tf_op jit(solution)/shard_map/all_gather | solution.py:144
  385.5 7.5 fusion.47
  393.0 35.9 %all-gather.16.cloned.1.call-done = bf16[768,768]{0,1:T(8,128)(2,1)} async-done(((bf16[768,96]{0,1:T(8,128)(2,1)}), bf16[768,768]{0,1:T(8,128)(2,1)}) %all-gather.16.cloned.1.call-update) | async-done | bytes 1179664 | tf_op jit(solution)/shard_map/all_gather | solution.py:81
  428.9 8.9 fusion.51
  437.9 20.6 %all-gather.18.cloned.1.call-done = bf16[2048,1,768]{2,0,1:T(8,128)(2,1)} async-done(((bf16[512,1,768]{2,0,1:T(8,128)(2,1)}), bf16[2048,1,768]{2,0,1:T(8,128)(2,1)}) %all-gather.18.cloned.1.call-update) | async-done | bytes 3145744 | tf_op jit(solution)/shard_map/all_gather | solution.py:174
  458.4 9.4 convert_reduce_fusion
  469.6 4.5 convolution_bitcast_fusion.3
  475.6 23.6 %reduce-scatter.15.cloned.1.call-done = bf16[512,1,768]{2,0,1:T(8,128)(2,1)} async-done(((bf16[2048,1,768]{2,0,1:T(8,128)(2,1)}), bf16[512,1,768]{2,0,1:T(8,128)(2,1)}) %reduce-scatter.15.cloned.1.call-update) | async-done | bytes 786448 | tf_op jit(solution)/shard_map/reduce_scatter | solution.py:151
  499.1 60.9 %reduce-scatter.17.cloned.1.call-done = f32[512,1,768]{2,0,1:T(8,128)} async-done(((f32[2048,1,768]{2,0,1:T(8,128)}), f32[512,1,768]{2,0,1:T(8,128)}) %reduce-scatter.17.cloned.1.call-update) | async-done | bytes 1572880 | tf_op jit(solution)/shard_map/reduce_scatter | solution.py:184
  560.1 4.8 multiply_reduce_fusion.2
  572.7 17.7 %collective-permute-done = bf16[512,1,768]{2,0,1:T(8,128)(2,1)S(1)} collective-permute-done((bf16[512,1,768]{2,0,1:T(8,128)(2,1)}, bf16[512,1,768]{2,0,1:T(8,128)(2,1)S(1)}, u32[]{:S(2)}, u32[]{:S(2)}) %collective-permute-start) | collective-permute-done | bytes 786464 | tf_op jit(solution)/shard_map/ppermute | solution.py:202
  592.4 9.5 collective-permute-done.2
  608.3 110.2 %while.31 = (s32[]{:T(128)}, f32[1,3,2048,64]{2,3,1,0:T(8,128)S(1)}, f32[1,3,2048,64]{2,3,1,0:T(8,128)}, f32[4,3,512,64]{2,3,1,0:T(8,128)}, s32[4]{0:T(128)S(1)}...) while((s32[]{:T(128)}, ...), condition=%wide.region_15.16_spmd, body=%wide.region_13.15_spmd.sunk | while | flops 2042362368 | bytes 129411448 | solution.py:253
  614.3 4.9 fusion.146
  623.2 4.5 multiply_convert_fusion.7
  627.8 5.7 fusion.147
  641.9 4.9 fusion.146
  650.8 4.5 multiply_convert_fusion.7
  655.3 5.7 fusion.147
  669.4 4.9 fusion.146
  678.3 4.5 multiply_convert_fusion.7
  682.9 5.7 fusion.147
  697.0 4.9 fusion.146
  705.9 4.5 multiply_convert_fusion.7
  710.4 5.7 fusion.147
  726.4 4.5 convolution_bitcast_fusion.1
  736.2 4.6 fusion.79
  743.7 4.8 reshape.592
  749.2 9.5 fusion.41
  758.7 6.9 fusion.45
  766.3 22.9 %reduce-scatter.19.cloned.1.call-done = f32[512,1,768]{2,0,1:T(8,128)} async-done(((f32[2048,1,768]{2,0,1:T(8,128)}), f32[512,1,768]{2,0,1:T(8,128)}) %reduce-scatter.19.cloned.1.call-update) | async-done | bytes 1572880 | tf_op jit(solution)/shard_map/reduce_scatter | solution.py:274
  798.2 56.8 %reduce-scatter.27.cloned.1.call-done = f32[96,192]{1,0:T(8,128)} async-done(((f32[768,192]{1,0:T(8,128)}), f32[96,192]{1,0:T(8,128)}) %reduce-scatter.27.cloned.1.call-update) | async-done | bytes 73744
  856.7 67.8 %reduce-scatter.25.cloned.1.call-done = f32[96,576]{1,0:T(8,128)} async-done(((f32[768,576]{1,0:T(8,128)}), f32[96,576]{1,0:T(8,128)}) %reduce-scatter.25.cloned.1.call-update) | async-done | bytes 221200
  931.8 41.5 %all-reduce.8 = (f32[8,128]{1,0:T(8,128)S(1)}, f32[4608]{0:T(1024)}, f32[768]{0:T(1024)}, f32[768]{0:T(1024)}, f32[3072]{0:T(1024)}, /*index=5*/f32[768]{0:T(1024)}, f32[3]{0:T(128)S(1)}) all-reduce(f32[8,128]{1,0:T(8,128)S(1)} %dynamic_update_slice.50, f32[4608]{0:T(1024)S(1)} %reduce.25, ...), channel_id=1, replica_groups=mesh['dp'=8,'tensor'=4] {'dp','tensor'}, use_global_device_ids=true, to_apply=%region_25.26 | all-reduce | flops 11011 | bytes 88088 | tf_op jit(solution)/shard_map/psum | solution.py:297
  974.3 22.7 %reduce-scatter.23.cloned.1.call-done = f32[768,96]{0,1:T(8,128)} async-done(((f32[768,768]{0,1:T(8,128)}), f32[768,96]{0,1:T(8,128)}) %reduce-scatter.23.cloned.1.call-update) | async-done | bytes 294928 | tf_op jit(solution)/shard_map/reduce_scatter | solution.py:287
  997.0 72.0 %reduce-scatter.21.cloned.1.call-done = f32[96,768]{1,0:T(8,128)} async-done(((f32[768,768]{1,0:T(8,128)}), f32[96,768]{1,0:T(8,128)}) %reduce-scatter.21.cloned.1.call-update) | async-done | bytes 294928 | tf_op jit(solution)/shard_map/reduce_scatter | solution.py:286
  1069.0 140.1 %all-reduce.12.cloned.1.call-done = f32[128,4608]{1,0:T(8,128)} async-done(((f32[128,4608]{1,0:T(8,128)}), f32[128,4608]{1,0:T(8,128)}) %all-reduce.12.cloned.1.call-update) | async-done | bytes 2359312 | tf_op jit(solution)/shard_map/psum | solution.py:297
  (311 shorter events, 183.0 us)
Async XLA Ops:
  7.2 49.4 %copy-start.57 = (bf16[1,128]{1,0:T(2,128)(2,1)S(1)}, bf16[1,128]{1,0:T(2,128)(2,1)}, u32[]{:S(2)}) copy-start(bf16[1,128]{1,0:T(2,128)(2,1)} %param.18) | copy-start | bytes 772
  7.2 51.8 %copy-start.3 = (bf16[512,1,768]{2,0,1:T(8,128)(2,1)S(1)}, bf16[512,1,768]{2,0,1:T(8,128)(2,1)}, u32[]{:S(2)}) copy-start(bf16[512,1,768]{2,0,1:T(8,128)(2,1)} %param.17) | copy-start | bytes 2359300
  7.2 49.4 %all-gather.8.cloned.1.call-start = ((), (), s32[]{:S(2)}) async-start(), calls=%async_computation.8 | async-start | bytes 1327104 | tf_op jit(solution)/shard_map/all_gather | solution.py:73
  7.9 125.7 %all-gather.10.cloned.1.call-start = ((), (), s32[]{:S(2)}) async-start(), calls=%async_computation.9 | async-start | bytes 3932160 | tf_op jit(solution)/shard_map/all_gather | solution.py:96
  53.7 6.6 copy-start.32
  55.0 5.3 copy-start.36
  56.6 3.8 copy-start.42
  56.6 3.9 copy-start.40
  59.0 508.2 %copy-start.38 = (f32[768]{0:T(1024)}, f32[768]{0:T(1024)S(1)}, u32[]{:S(2)}) copy-start(f32[768]{0:T(1024)S(1)} %get-tuple-element.319) | copy-start | bytes 9220
  60.3 252.4 %reduce-scatter.13.cloned.1.call-start = ((), (), s32[]{:S(2)}) async-start(), calls=%async_computation.10 | async-start | bytes 7864320 | tf_op jit(solution)/shard_map/reduce_scatter | solution.py:133
  97.1 36.5 %copy-start.25 = (bf16[3,768,192]{1,2,0:T(8,128)(2,1)S(1)}, bf16[3,768,192]{1,2,0:T(8,128)(2,1)}, u32[]{:S(2)}) copy-start(bf16[3,768,192]{1,2,0:T(8,128)(2,1)} %copy.50) | copy-start | bytes 2654212
  248.3 3.0 copy-start.22
  255.0 101.1 %all-gather.14.cloned.1.call-start = ((), (), s32[]{:S(2)}) async-start(), calls=%async_computation.12 | async-start | bytes 1327104 | tf_op jit(solution)/shard_map/all_gather | solution.py:79
  255.6 129.9 %all-gather.12.cloned.1.call-start = ((), (), s32[]{:S(2)}) async-start(), calls=%async_computation.11 | async-start | bytes 3932160 | tf_op jit(solution)/shard_map/all_gather | solution.py:144
  316.6 112.2 %all-gather.16.cloned.1.call-start = ((), (), s32[]{:S(2)}) async-start(), calls=%async_computation.13 | async-start | bytes 1327104 | tf_op jit(solution)/shard_map/all_gather | solution.py:81
  317.2 141.2 %all-gather.18.cloned.1.call-start = ((), (), s32[]{:S(2)}) async-start(), calls=%async_computation.15 | async-start | bytes 3932160 | tf_op jit(solution)/shard_map/all_gather | solution.py:174
  319.6 179.5 %reduce-scatter.15.cloned.1.call-start = ((), (), s32[]{:S(2)}) async-start(), calls=%async_computation.14 | async-start | bytes 3932160 | tf_op jit(solution)/shard_map/reduce_scatter | solution.py:151
  437.8 122.2 %reduce-scatter.17.cloned.1.call-start = ((), (), s32[]{:S(2)}) async-start(), calls=%async_computation.16 | async-start | bytes 7864320 | tf_op jit(solution)/shard_map/reduce_scatter | solution.py:184
  458.4 11.1 copy-start.59
  474.1 315.1 %reduce-scatter.19.cloned.1.call-start = ((), (), s32[]{:S(2)}) async-start(), calls=%async_computation.17 | async-start | bytes 7864320 | tf_op jit(solution)/shard_map/reduce_scatter | solution.py:274
  560.1 5.5 copy-start.12
  571.0 19.5 %collective-permute-start = (bf16[512,1,768]{2,0,1:T(8,128)(2,1)}, bf16[512,1,768]{2,0,1:T(8,128)(2,1)S(1)}, u32[]{:S(2)}, u32[]{:S(2)}) collective-permute-start(bf16[512,1,768]{2,0,1:T(8,128)(2,1)} %get-tuple-element.368), channel_id=1, source_target_pairs={{0,1},{1,2},{2,3},{3,0},{4,5},{5,6},{6,7},{7,4},{8,9},{9,10},{10,1... | collective-permute-start | bytes 2359304 | tf_op jit(solution)/shard_map/ppermute | solution.py:202
  571.0 20.4 %collective-permute-start.1 = (bf16[512,1,768]{2,0,1:T(8,128)(2,1)}, bf16[512,1,768]{2,0,1:T(8,128)(2,1)S(1)}, u32[]{:S(2)}, u32[]{:S(2)}) collective-permute-start(bf16[512,1,768]{2,0,1:T(8,128)(2,1)} %get-tuple-element.368), channel_id=1, source_target_pairs={{0,3},{1,0},{2,1},{3,2},{4,7},{5,4},{6,5},{7,6},{8,11},{9,8},{10,9... | collective-permute-start | bytes 2359304 | tf_op jit(solution)/shard_map/ppermute | solution.py:205
  590.5 11.4 collective-permute-start.2
  627.8 5.7 copy-start
  655.3 5.7 copy-start
  682.9 5.7 copy-start
  710.4 5.7 copy-start
  721.7 3.5 copy-start.30
  730.9 5.3 copy-start.28
  730.9 124.1 %reduce-scatter.27.cloned.1.call-start = ((), (), s32[]{:S(2)}) async-start(), calls=%async_computation.22 | async-start | bytes 884736
  736.2 188.3 %reduce-scatter.25.cloned.1.call-start = ((), (), s32[]{:S(2)}) async-start(), calls=%async_computation.21 | async-start | bytes 2211840
  748.5 248.5 %reduce-scatter.23.cloned.1.call-start = ((), (), s32[]{:S(2)}) async-start(), calls=%async_computation.20 | async-start | bytes 2654208 | tf_op jit(solution)/shard_map/reduce_scatter | solution.py:287
  758.7 310.3 %reduce-scatter.21.cloned.1.call-start = ((), (), s32[]{:S(2)}) async-start(), calls=%async_computation.19 | async-start | bytes 2654208 | tf_op jit(solution)/shard_map/reduce_scatter | solution.py:286
  765.6 23.5 %copy-start.4 = (bf16[512,1,768]{2,0,1:T(8,128)(2,1)S(1)}, bf16[512,1,768]{2,0,1:T(8,128)(2,1)}, u32[]{:S(2)}) copy-start(bf16[512,1,768]{2,0,1:T(8,128)(2,1)} %param.17) | copy-start | bytes 2359300
  765.6 23.5 %copy-start.33 = (f32[768]{0:T(1024)S(1)}, f32[768]{0:T(1024)}, u32[]{:S(2)}) copy-start(f32[768]{0:T(1024)} %copy-done.32) | copy-start | bytes 9220
  765.7 23.5 %copy-start.35 = (f32[768]{0:T(1024)S(1)}, f32[768]{0:T(1024)}, u32[]{:S(2)}) copy-start(f32[768]{0:T(1024)} %copy-done.34) | copy-start | bytes 9220
  765.7 23.5 %copy-start.37 = (f32[512]{0:T(512)S(1)}, f32[512]{0:T(512)}, u32[]{:S(2)}) copy-start(f32[512]{0:T(512)} %copy-done.36) | copy-start | bytes 6148
  765.7 26.7 %copy-start.13 = (f32[512,1,768]{2,0,1:T(8,128)S(1)}, f32[512,1,768]{2,0,1:T(8,128)}, u32[]{:S(2)}) copy-start(f32[512,1,768]{2,0,1:T(8,128)} %reduce-scatter.13.cloned.1.call-done) | copy-start | bytes 4718596
  765.7 25.5 %copy-start.45 = (f32[512]{0:T(512)S(1)}, f32[512]{0:T(512)}, u32[]{:S(2)}) copy-start(f32[512]{0:T(512)} %copy-done.44) | copy-start | bytes 6148
  765.7 25.5 %copy-start.43 = (f32[512]{0:T(512)S(1)}, f32[512]{0:T(512)}, u32[]{:S(2)}) copy-start(f32[512]{0:T(512)} %copy-done.42) | copy-start | bytes 6148
  765.7 443.4 %all-reduce.12.cloned.1.call-start = ((), (), s32[]{:S(2)}) async-start(), calls=%async_computation.18 | async-start | bytes 4718592 | tf_op jit(solution)/shard_map/psum | solution.py:297
  792.8 2.8 copy-start.53
  792.8 2.8 copy-start.52
  792.8 2.8 copy-start.51
  797.4 129.0 %copy-start.14 = (f32[512,1,768]{2,0,1:T(8,128)S(1)}, f32[512,1,768]{2,0,1:T(8,128)}, u32[]{:S(2)}) copy-start(f32[512,1,768]{2,0,1:T(8,128)} %get-tuple-element.380) | copy-start | bytes 4718596
  926.4 5.4 copy-start.49
  926.4 5.4 copy-start.50
  (34 other events, 46.6 us)
Sparse Core Ops, SparseCore 0:
  10.2 44.0 all-gather.7
  60.4 25.7 all-gather.9
  255.1 57.5 reduce-scatter.12
  315.0 41.0 all-gather.13
  358.2 27.2 all-gather.11
  387.8 41.0 all-gather.15
  431.1 27.2 all-gather.17
  461.1 37.9 reduce-scatter.14
  501.7 58.3 reduce-scatter.16
  731.0 58.0 reduce-scatter.18
  792.5 62.5 reduce-scatter.26
  858.8 65.6 reduce-scatter.24
  928.6 68.4 reduce-scatter.22
  1001.0 67.9 reduce-scatter.20
  1075.0 134.1 all-reduce.11
